TPU v7x, 128 devices: a whole 4x4x4 slice. The times are simulated.
128 devices in a mesh: dp: 16 (over z, y), mp: 8 (over x, core).
Axes of the slice: x: 4, y: 4, z: 4, core: 2. Of those that a mesh axis runs over, the one named last changes fastest.
Arguments:
- tokens: bfloat16 [32768, 1536], P(('dp', 'mp')), may hold values from -6 to 6
- lengths: int32 [16, 4], P('dp'), may hold values from 1 to 1024, 2048 in all within a row
- request_adapter: int32 [16, 4], P('dp'), may hold values from 0 to 15
- group_page_slots: int32 [16, 16], P('dp'), may hold values from 0 to 15, as said below
- routes: int32 [32768, 4], P(('dp', 'mp')), may hold values from 0 to 31, all different within a row; in each aligned block of 256 rows (0 to 255, 256 to 511, ...) at most 48 rows name the same one
- attention_gain: float32 [1536], replicated, may hold values from 0.1 to 1.9
- query_key_value_weight: bfloat16 [1536, 2048], P(None, 'mp')
- adapter_down_weight: bfloat16 [16, 1536, 16], P('dp'), may hold values from -0.15625 to 0.15625
- adapter_up_weight: bfloat16 [16, 16, 1536], P('dp'), may hold values from -0.75 to 0.75
- output_weight: bfloat16 [1536, 1536], P(None, 'mp'), may hold values from -0.15625 to 0.15625
- expert_norm_gain: float32 [1536], replicated, may hold values from 0.1 to 1.9
- router: bfloat16 [1536, 32], replicated, may hold values from -0.3125 to 0.3125
- expert_gate_up_weight: bfloat16 [32, 1536, 1536], P('dp'), may hold values from -0.15625 to 0.15625
- expert_down_weight: bfloat16 [32, 768, 1536], P('dp'), may hold values from -0.21875 to 0.21875
Outputs:
- layer_out: bfloat16 [32768, 1536], P(('dp', 'mp'))
- kv_pool: bfloat16 [256, 128, 512], P(('dp', 'mp'))
Inputs may be any that keep to these rules, and one draw needn't show every extreme that they name: `lengths`: each row sums to 2048, and its longest length is exactly half of 2048. `group_page_slots`: each row is a permutation of the 16 slots of its group. `routes`: A token names 4 different experts; among the rows of one device no expert is named more than 48 times.
All inputs are finite; a program needn't handle non-finite values.
Results may differ from a plain program's by a relative error of at most 0.02.
The roundings to bfloat16 on the way count: a program that leaves them out, or rounds other values in their place, can miss the bound.
Values may be sent and summed in bfloat16 or wider, within the bound.
A program may use at most 128 MiB of HBM per device.

v0:
```python
import jax
import jax.numpy as jnp
from jax import lax
from jax.sharding import PartitionSpec as P

HEAD_SIZE = 128
PAGE = 128
CAP = 48
eps = 1e-06
neg_fill = -1e30


def rms_norm(values, gains):
    widened = values.astype(jnp.float32)
    inv_rms = lax.rsqrt(jnp.mean(widened * widened, axis=-1, keepdims=True) + eps)
    return (widened * inv_rms * gains).astype(jnp.bfloat16)


def segment_ids(length_row, offset, count):
    seq_ends = jnp.cumsum(length_row)
    positions = offset + jnp.arange(count, dtype=jnp.int32)
    return jnp.sum((positions[:, None] >= seq_ends[None, :]).astype(jnp.int32), axis=1)


def shards(
    tokens,
    lengths,
    request_adapter,
    group_page_slots,
    routes,
    attention_gain,
    query_key_value_weight,
    adapter_down_weight,
    adapter_up_weight,
    output_weight,
    expert_norm_gain,
    router,
    expert_gate_up_weight,
    expert_down_weight,
):
    adapter_down_map, adapter_up_map = (
        lax.all_gather(adapter_down_weight, "dp", axis=0, tiled=True),
        lax.all_gather(adapter_up_weight, "dp", axis=0, tiled=True),
    )
    tokens_per_shard = tokens.shape[0]
    model_columns = tokens.shape[1]
    mp_index = lax.axis_index("mp")
    group_start = mp_index * tokens_per_shard
    length_row = lengths[0]
    query_seg = segment_ids(length_row, group_start, tokens_per_shard)
    normalized_input = rms_norm(tokens, attention_gain)
    full_qkv, full_out = (
        lax.all_gather(query_key_value_weight, "mp", axis=1, tiled=True),
        lax.all_gather(output_weight, "mp", axis=1, tiled=True),
    )
    complete_query_key_value = jnp.dot(
        normalized_input, full_qkv, preferred_element_type=jnp.float32
    )
    seq_count = lengths.shape[1]
    seq_match = (query_seg[:, None] == jnp.arange(seq_count, dtype=jnp.int32)[None, :]).astype(
        jnp.int32
    )
    token_adapter = jnp.sum(seq_match * request_adapter[0][None, :], axis=1)
    adapter_total = adapter_down_map.shape[0]
    adapter_rank_size = adapter_down_map.shape[2]
    query_width = adapter_up_map.shape[2]
    flattened_down = jnp.transpose(adapter_down_map, (1, 0, 2)).reshape(
        model_columns, adapter_total * adapter_rank_size
    )
    adapter_middle = jnp.dot(
        normalized_input, flattened_down, preferred_element_type=jnp.float32
    ).reshape(tokens_per_shard, adapter_total, adapter_rank_size)
    adapter_selected = token_adapter[:, None] == jnp.arange(adapter_total, dtype=jnp.int32)[None, :]
    adapter_middle = (
        jnp.where(adapter_selected[:, :, None], adapter_middle, 0.0)
        .astype(jnp.bfloat16)
        .reshape(tokens_per_shard, adapter_total * adapter_rank_size)
    )
    adapter_query = jnp.dot(
        adapter_middle,
        adapter_up_map.reshape(adapter_total * adapter_rank_size, query_width),
        preferred_element_type=jnp.float32,
    )
    query_rows = (complete_query_key_value[:, :query_width] + adapter_query).astype(jnp.bfloat16)
    key_value = complete_query_key_value[:, query_width:].astype(jnp.bfloat16)
    kv_dim = key_value.shape[1] // 2
    group_kv = lax.all_gather(key_value, "mp", axis=0, tiled=True)
    group_len = group_kv.shape[0]
    key_seg = segment_ids(length_row, 0, group_len)
    key_pos = jnp.arange(group_len, dtype=jnp.int32)
    query_pos = group_start + jnp.arange(tokens_per_shard, dtype=jnp.int32)
    allowed = (query_seg[:, None] == key_seg[None, :]) & (key_pos[None, :] <= query_pos[:, None])
    n_kv = kv_dim // HEAD_SIZE
    group_share = query_width // kv_dim
    pieces = []
    for head_position in range(n_kv):
        lo_col = head_position * group_share * HEAD_SIZE
        q_head = query_rows[:, lo_col : lo_col + group_share * HEAD_SIZE].reshape(
            tokens_per_shard, group_share, HEAD_SIZE
        )
        k_head = group_kv[:, head_position * HEAD_SIZE : (head_position + 1) * HEAD_SIZE]
        v_head = group_kv[
            :, kv_dim + head_position * HEAD_SIZE : kv_dim + (head_position + 1) * HEAD_SIZE
        ]
        scores = jnp.einsum(
            "tgd,sd->tgs", q_head, k_head, preferred_element_type=jnp.float32
        ) * HEAD_SIZE ** (-0.5)
        scores = jnp.where(allowed[:, None, :], scores, neg_fill)
        row_max = jnp.max(scores, axis=2, keepdims=True)
        expd = jnp.exp(scores - row_max)
        probs = (expd / jnp.sum(expd, axis=2, keepdims=True)).astype(jnp.bfloat16)
        mixed = jnp.einsum("tgs,sd->tgd", probs, v_head, preferred_element_type=jnp.float32)
        pieces.append(mixed.astype(jnp.bfloat16).reshape(tokens_per_shard, group_share * HEAD_SIZE))
    attended = jnp.concatenate(pieces, axis=1)
    projected = jnp.dot(attended, full_out, preferred_element_type=jnp.float32)
    residual = (tokens.astype(jnp.float32) + projected).astype(jnp.bfloat16)
    pages_dev = tokens_per_shard // PAGE
    pages_grp = group_page_slots.shape[1]
    my_slots = mp_index * pages_dev + jnp.arange(pages_dev, dtype=jnp.int32)
    slot_match = (group_page_slots[0][None, :] == my_slots[:, None]).astype(jnp.int32)
    source_page = jnp.sum(slot_match * jnp.arange(pages_grp, dtype=jnp.int32)[None, :], axis=1)
    pool = group_kv.reshape(pages_grp, PAGE, 2 * kv_dim)[source_page]
    ffn_in = rms_norm(residual, expert_norm_gain)
    logits = jnp.dot(ffn_in, router, preferred_element_type=jnp.float32)
    chosen = jnp.take_along_axis(logits, routes, axis=1)
    route_weights = jax.nn.softmax(chosen, axis=1)
    n_exp = router.shape[1]
    top_k = routes.shape[1]
    pair_expert = routes.reshape(-1)
    expert_hits = (pair_expert[:, None] == jnp.arange(n_exp, dtype=jnp.int32)[None, :]).astype(
        jnp.int32
    )
    slot_index = jnp.sum((jnp.cumsum(expert_hits, axis=0) - 1) * expert_hits, axis=1)
    target = pair_expert * CAP + slot_index
    send_rows = (
        jnp.zeros((n_exp * CAP, model_columns), jnp.bfloat16)
        .at[target]
        .set(jnp.repeat(ffn_in, top_k, axis=0))
    )
    n_dp = lax.axis_size("dp")
    exp_local = n_exp // n_dp
    outgoing = send_rows.reshape(n_dp, exp_local, CAP, model_columns)
    arrived = lax.all_to_all(outgoing, "dp", split_axis=0, concat_axis=0, tiled=True)
    gate_up = jnp.einsum(
        "secd,edf->secf", arrived, expert_gate_up_weight, preferred_element_type=jnp.float32
    )
    hidden_units = expert_down_weight.shape[1]
    active = (jnp.maximum(gate_up[..., :hidden_units], 0.0) * gate_up[..., hidden_units:]).astype(
        jnp.bfloat16
    )
    produced = jnp.einsum(
        "secf,efd->secd", active, expert_down_weight, preferred_element_type=jnp.float32
    ).astype(jnp.bfloat16)
    returned = lax.all_to_all(produced, "dp", split_axis=0, concat_axis=0, tiled=True)
    pair_out = (
        returned.reshape(n_exp * CAP, model_columns)[target]
        .astype(jnp.float32)
        .reshape(tokens_per_shard, top_k, model_columns)
    )
    mixture = jnp.sum(pair_out * route_weights[:, :, None], axis=1)
    layer_out = (residual.astype(jnp.float32) + mixture).astype(jnp.bfloat16)
    return (layer_out, pool)


def solution(mesh):
    return jax.shard_map(
        shards,
        mesh=mesh,
        in_specs=(
            P(("dp", "mp"), None),
            P("dp", None),
            P("dp", None),
            P("dp", None),
            P(("dp", "mp"), None),
            P(),
            P(None, "mp"),
            P("dp", None, None),
            P("dp", None, None),
            P(None, "mp"),
            P(),
            P(),
            P("dp", None, None),
            P("dp", None, None),
        ),
        out_specs=(P(("dp", "mp"), None), P(("dp", "mp"), None, None)),
        check_vma=False,
    )
```

profile of v0, /device:TPU:6, one launch (start us, length us, event | category | flops | bytes accessed | tf_op | source)
XLA Modules:
  0.0 358.5 jit_solution(10791619385420463547)
XLA Ops:
  9.4 46.9 %all-gather.4.cloned.1.call-done = bf16[1536,2048]{1,0:T(8,128)(2,1)} async-done(((bf16[1536,256]{1,0:T(8,128)(2,1)}), bf16[1536,2048]{1,0:T(8,128)(2,1)}) %all-gather.4.cloned.1.call-update) | async-done | bytes 6291472 | tf_op jit(solution)/shard_map/all_gather | solution.py:53
  56.3 4.9 %fusion.49 = f32[256,2048]{1,0:T(8,128)S(1)} fusion(bf16[1536,2048]{1,0:T(8,128)(2,1)} %all-gather.4.cloned.1.call-done, bf16[256,1536]{1,0:T(8,128)(2,1)} %param.14, f32[1536]{0:T(1024)} %param.19, f32[256]{0:T(256)S(1)} %add_rsqrt_fusion.1), kind=kOutput, calls=%fused_computation.68 | convolution fusion | flops 1612185600 | bytes 9182208 | tf_op jit(solution)/shard_map/dot_general | solution.py:56
  65.0 25.1 %all_gather.16 = bf16[16,1536,16]{1,2,0:T(8,128)(2,1)S(1)} all-gather(bf16[1,1536,16]{1,2,0:T(8,128)(2,1)S(1)} %copy-done.9), channel_id=1, replica_groups=mesh['dp'=16,'mp'=8] {'dp'}, dimensions={0}, use_global_device_ids=true | all-gather | bytes 835584 | tf_op jit(solution)/shard_map/all_gather | solution.py:42
  90.1 9.0 %reduce-window.19 = s32[32,8,128]{2,1,0:T(8,128)S(1)} reduce-window(s32[32,8,128]{2,1,0:T(8,128)S(1)} %fusion.54, s32[]{:T(128)} %constant.20.clone.1), window={size=1x1x128 pad=0_0x0_0x127_0}, to_apply=%region_9.10 | reduce-window | flops 4161536 | bytes 262148 | tf_op jit(solution)/shard_map/reduce-window.1
  99.9 23.2 %all_gather.17 = bf16[16,16,1536]{2,1,0:T(8,128)(2,1)S(1)} all-gather(bf16[1,16,1536]{2,1,0:T(8,128)(2,1)S(1)} %copy-done.10), channel_id=1, replica_groups=mesh['dp'=16,'mp'=8] {'dp'}, dimensions={0}, use_global_device_ids=true | all-gather | bytes 835584 | tf_op jit(solution)/shard_map/all_gather | solution.py:43
  125.3 2.6 fusion.26
  128.4 7.3 %fusion.46 = f32[256,6,2048]{2,0,1:T(8,128)} fusion(bf16[256,6,128]{0,2,1:T(8,128)(2,1)S(1)} %bitcast.93, bf16[2048,512]{1,0:T(8,128)(2,1)} %all-gather.6.cloned.1.call-done), kind=kOutput, calls=%fused_computation.66 | convolution fusion | flops 805306368 | bytes 13500416 | tf_op jit(solution)/shard_map/tgd,sd->tgs/dot_general | solution.py:105
  135.7 2.9 fusion.45
  138.6 17.6 %fusion.70 = (f32[256,6]{0,1:T(8,128)S(1)}, f32[256,6,2048]{2,0,1:T(8,128)}) fusion(f32[256,6,2048]{2,0,1:T(8,128)} %fusion.46, pred[256,2048]{1,0:T(8,128)(4,1)} %fusion.31), kind=kOutput, calls=%fused_computation.112 | output fusion | flops 18876416 | bytes 25696256 | tf_op jit(solution)/shard_map/sub | solution.py:110
  156.2 9.5 %fusion.69 = (f32[256,6]{0,1:T(8,128)S(1)}, f32[256,6,2048]{2,0,1:T(8,128)}) fusion(f32[256,6,2048]{2,0,1:T(8,128)S(1)} %fusion.45, pred[256,2048]{1,0:T(8,128)(4,1)} %fusion.31), kind=kOutput, calls=%fused_computation.111 | output fusion | flops 18876416 | bytes 25696256 | tf_op jit(solution)/shard_map/sub | solution.py:110
  165.7 7.0 %fusion.36 = bf16[256,6,128]{0,2,1:T(8,128)(2,1)S(1)} fusion(f32[256,6,2048]{2,0,1:T(8,128)} %get-tuple-element.9, f32[256,6]{0,1:T(8,128)S(1)} %get-tuple-element.8, bf16[2048,512]{1,0:T(8,128)(2,1)} %all-gather.6.cloned.1.call-done), kind=kOutput, calls=%fused_computation.53 | convolution fusion | flops 811794432 | bytes 13506560 | tf_op jit(solution)/shard_map/tgs,sd->tgd/dot_general | solution.py:112
  174.0 3.7 %fusion.35 = bf16[256,6,128]{0,2,1:T(8,128)(2,1)S(1)} fusion(f32[256,6,2048]{2,0,1:T(8,128)S(1)} %copy-done.18, f32[256,6]{0,1:T(8,128)S(1)} %get-tuple-element.6, bf16[2048,512]{1,0:T(8,128)(2,1)} %all-gather.6.cloned.1.call-done), kind=kOutput, calls=%fused_computation.52 | convolution fusion | flops 811794432 | bytes 13506560 | tf_op jit(solution)/shard_map/tgs,sd->tgd/dot_general | solution.py:112
  177.7 3.9 %multiply_reduce_fusion.1 = (f32[256]{0:T(256)S(1)}, f32[256,1536]{1,0:T(8,128)S(1)}) fusion(bf16[1536,1536]{0,1:T(8,128)(2,1)} %all-gather.8.cloned.1.call-done, bf16[256,768]{0,1:T(8,128)(2,1)S(1)} %bitcast.107, bf16[256,768]{0,1:T(8,128)(2,1)S(1)} %bitcast.106, bf16[256,1536]{1,0:T(8,128)(2,1)S(1)} %copy-done.6), kind=kOutput, calls=%fused_computation.51 | convolution fusion | flops 1211891456 | bytes 7865344 | tf_op jit(solution)/shard_map/dot_general | solution.py:115
  187.3 9.2 %scatter_custom_fusion = bf16[1536,1536]{1,0:T(8,128)(2,1)} fusion(s32[1024]{0:T(1024)S(1)} %bitcast.99, bf16[1024,1536]{1,0:T(8,128)(2,1)} %reshape.285, bf16[]{:T(256)} %constant.34.clone.1), kind=kCustom, calls=%fused_computation.42 | custom fusion | bytes 4719104 | tf_op jit(solution)/shard_map/scatter | solution.py:138
  196.5 54.8 %all_to_all.10 = bf16[16,2,48,1536]{3,2,1,0:T(8,128)(2,1)S(1)} all-to-all(bf16[16,2,48,1536]{3,2,1,0:T(8,128)(2,1)} %bitcast.92), channel_id=1, replica_groups=mesh['dp'=16,'mp'=8] {'dp'}, dimensions={0} | all-to-all | bytes 9437184 | tf_op jit(solution)/shard_map/all_to_all | solution.py:143
  251.3 10.0 %fusion.14 = f32[16,2,48,1536]{3,2,0,1:T(8,128)S(1)} fusion(bf16[2,1536,1536]{2,1,0:T(8,128)(2,1)} %param.26, bf16[16,2,48,1536]{3,2,1,0:T(8,128)(2,1)S(1)} %all_to_all.10), kind=kOutput, calls=%fused_computation.25 | convolution fusion | flops 7247757312 | bytes 23592960 | tf_op jit(solution)/shard_map/secd,edf->secf/dot_general | solution.py:144
  261.2 6.4 %convert_bitcast_fusion = bf16[16,2,48,1536]{3,2,0,1:T(8,128)(2,1)S(1)} fusion(bf16[2,768,1536]{2,1,0:T(8,128)(2,1)} %param.27, f32[16,2,48,1536]{3,2,0,1:T(8,128)S(1)} %fusion.14), kind=kOutput, calls=%fused_computation.32 | convolution fusion | flops 3629776896 | bytes 18874368 | tf_op jit(solution)/shard_map/secf,efd->secd/dot_general | solution.py:151
  270.2 4.9 %all-to-all-start.1 = ((bf16[16,2,48,1536]{3,2,1,0:T(8,128)(2,1)}), bf16[16,2,48,1536]{3,2,1,0:T(8,128)(2,1)}, u32[]{:S(2)}, u32[]{:S(2)}) async-start(bf16[16,2,48,1536]{3,2,1,0:T(8,128)(2,1)} %copy.87), calls=%async_computation.1 | async-start | bytes 9437184 | tf_op jit(solution)/shard_map/all_to_all | solution.py:154
  276.0 8.7 %gather_fusion.2 = f32[1024]{0:T(1024)S(1)} fusion(f32[256,32]{0,1:T(8,128)S(1)} %fusion.71, s32[1024]{0:T(1024)S(1)} %reshape.275), kind=kCustom, calls=%fused_computation.2 | custom fusion | bytes 16384 | tf_op jit(solution)/shard_map/jit(take_along_axis)/gather | solution.py:125
  285.1 2.9 gather_fusion.1
  288.0 41.7 %all-to-all-done.1 = bf16[16,2,48,1536]{3,2,1,0:T(8,128)(2,1)} async-done(((bf16[16,2,48,1536]{3,2,1,0:T(8,128)(2,1)}), bf16[16,2,48,1536]{3,2,1,0:T(8,128)(2,1)}, u32[]{:S(2)}, u32[]{:S(2)}) %all-to-all-start.1) | async-done | bytes 4718624 | tf_op jit(solution)/shard_map/all_to_all | solution.py:154
  329.7 9.6 %gather_fusion = bf16[1024,1536]{1,0:T(8,128)(2,1)S(1)} fusion(bf16[1536,1536]{1,0:T(8,128)(2,1)} %bitcast.28, s32[1024]{0:T(1024)S(1)} %broadcast_clamp_fusion), kind=kCustom, calls=%fused_computation | custom fusion | bytes 6295552 | tf_op jit(solution)/shard_map/gather | solution.py:156
  339.3 3.9 %reshape.258 = f32[256,4,1536]{2,1,0:T(4,128)} reshape(bf16[1024,1536]{1,0:T(8,128)(2,1)S(1)} %gather_fusion) | data formatting | bytes 9437184 | tf_op jit(solution)/shard_map/convert_element_type | solution.py:157
  343.1 7.5 %multiply_reduce_fusion = f32[256,1536]{1,0:T(8,128)S(1)} fusion(f32[256,4,1536]{2,1,0:T(4,128)} %reshape.258, f32[256,4]{1,0:T(8,128)S(1)} %copy.90), kind=kLoop, calls=%fused_computation.16 | loop fusion | flops 2752512 | bytes 7868416 | tf_op jit(solution)/shard_map/reduce_sum | solution.py:160
  (95 shorter events, 20.9 us)
Async XLA Ops:
  7.2 268.5 %copy-start = (bf16[1536,32]{0,1:T(8,128)(2,1)S(1)}, bf16[1536,32]{0,1:T(8,128)(2,1)}, u32[]{:S(2)}) copy-start(bf16[1536,32]{0,1:T(8,128)(2,1)} %param.25) | copy-start | bytes 294916
  7.2 49.2 %all-gather.4.cloned.1.call-start = ((), (), s32[]{:S(2)}) async-start(), calls=%async_computation.2 | async-start | bytes 7077888 | tf_op jit(solution)/shard_map/all_gather | solution.py:53
  7.9 120.4 %all-gather.6.cloned.1.call-start = ((), (), s32[]{:S(2)}) async-start(), calls=%async_computation.3 | async-start | bytes 2359296 | tf_op jit(solution)/shard_map/all_gather | solution.py:87
  9.3 54.8 %copy-start.7 = (s32[256,4]{0,1:T(4,128)S(1)}, s32[256,4]{0,1:T(4,128)}, u32[]{:S(2)}) copy-start(s32[256,4]{0,1:T(4,128)} %param.18) | copy-start | bytes 12292
  9.3 55.2 %copy-start.16 = (s32[1,4]{1,0:T(1,128)S(1)}, s32[1,4]{1,0:T(1,128)}, u32[]{:S(2)}) copy-start(s32[1,4]{1,0:T(1,128)} %param.15) | copy-start | bytes 52
  9.4 55.5 %copy-start.14 = (s32[1,4]{1,0:T(1,128)S(1)}, s32[1,4]{1,0:T(1,128)}, u32[]{:S(2)}) copy-start(s32[1,4]{1,0:T(1,128)} %param.16) | copy-start | bytes 52
  9.4 55.6 %copy-start.9 = (bf16[1,1536,16]{1,2,0:T(8,128)(2,1)S(1)}, bf16[1,1536,16]{1,2,0:T(8,128)(2,1)}, u32[]{:S(2)}) copy-start(bf16[1,1536,16]{1,2,0:T(8,128)(2,1)} %param.21) | copy-start | bytes 147460
  9.4 90.5 %copy-start.10 = (bf16[1,16,1536]{2,1,0:T(8,128)(2,1)S(1)}, bf16[1,16,1536]{2,1,0:T(8,128)(2,1)}, u32[]{:S(2)}) copy-start(bf16[1,16,1536]{2,1,0:T(8,128)(2,1)} %param.22) | copy-start | bytes 147460
  61.2 1.4 copy-start.11
  62.6 62.7 %copy-start.5 = (bf16[256,1536]{1,0:T(8,128)(2,1)S(1)}, bf16[256,1536]{1,0:T(8,128)(2,1)}, u32[]{:S(2)}) copy-start(bf16[256,1536]{1,0:T(8,128)(2,1)} %param.14) | copy-start | bytes 2359300
  62.6 62.7 %copy-start.15 = (f32[1536]{0:T(1024)S(1)}, f32[1536]{0:T(1024)}, u32[]{:S(2)}) copy-start(f32[1536]{0:T(1024)} %param.19) | copy-start | bytes 18436
  63.4 114.4 %all-gather.8.cloned.1.call-start = ((), (), s32[]{:S(2)}) async-start(), calls=%async_computation.4 | async-start | bytes 5308416 | tf_op jit(solution)/shard_map/all_gather | solution.py:54
  165.7 8.3 %copy-start.18 = (f32[256,6,2048]{2,0,1:T(8,128)S(1)}, f32[256,6,2048]{2,0,1:T(8,128)}, u32[]{:S(2)}) copy-start(f32[256,6,2048]{2,0,1:T(8,128)} %get-tuple-element.7) | copy-start | bytes 37748740
  174.0 3.7 %copy-start.6 = (bf16[256,1536]{1,0:T(8,128)(2,1)S(1)}, bf16[256,1536]{1,0:T(8,128)(2,1)}, u32[]{:S(2)}) copy-start(bf16[256,1536]{1,0:T(8,128)(2,1)} %param.14) | copy-start | bytes 2359300
  177.7 5.1 %copy-start.13 = (f32[1536]{0:T(1024)S(1)}, f32[1536]{0:T(1024)}, u32[]{:S(2)}) copy-start(f32[1536]{0:T(1024)} %param.24) | copy-start | bytes 18436
  181.6 1.2 copy-start.3
  183.0 0.9 copy-start.1
  183.9 3.4 copy-start.12
  270.2 4.9 %copy-start.8 = (s32[256,4]{0,1:T(4,128)S(1)}, s32[256,4]{0,1:T(4,128)}, u32[]{:S(2)}) copy-start(s32[256,4]{0,1:T(4,128)} %param.18) | copy-start | bytes 12292
  270.2 5.2 %copy-start.17 = (s32[1,16]{1,0:T(1,128)S(1)}, s32[1,16]{1,0:T(1,128)}, u32[]{:S(2)}) copy-start(s32[1,16]{1,0:T(1,128)} %param.17) | copy-start | bytes 196
  270.2 5.5 %copy-start.2 = (bf16[256,1536]{1,0:T(8,128)(2,1)S(1)}, bf16[256,1536]{1,0:T(8,128)(2,1)}, u32[]{:S(2)}) copy-start(bf16[256,1536]{1,0:T(8,128)(2,1)} %copy-done.1) | copy-start | bytes 2359300
  270.2 59.4 %all-to-all-start.1 = ((bf16[16,2,48,1536]{3,2,1,0:T(8,128)(2,1)}), bf16[16,2,48,1536]{3,2,1,0:T(8,128)(2,1)}, u32[]{:S(2)}, u32[]{:S(2)}) async-start(bf16[16,2,48,1536]{3,2,1,0:T(8,128)(2,1)} %copy.87), calls=%async_computation.1 | async-start | bytes 9437184 | tf_op jit(solution)/shard_map/all_to_all | solution.py:154
  343.1 7.5 %copy-start.4 = (f32[256,1536]{1,0:T(8,128)S(1)}, f32[256,1536]{1,0:T(8,128)}, u32[]{:S(2)}) copy-start(f32[256,1536]{1,0:T(8,128)} %copy-done.3) | copy-start | bytes 4718596
Sparse Core Ops, SparseCore 0:
  9.7 46.5 all-gather.3
  63.5 25.8 all-gather.5
  91.0 33.7 all-gather.7
where the time goes:
time: 365 us; the launch traced here: 358 us
  blocking collectives  103 us (28%)
  waiting for transfers between devices  90.1 us (25%)
  other arithmetic  49.3 us (14%)
  matrix products  49 us (13%)
  local copies, waits for them, and re-layouts  47.6 us (13%)
  between operations  14.4 us (4%)
  starting transfers between devices  5.02 us (1%)
    all_to_all x1, blocking collectives, shards(): lax.all_to_all(outgoing, 'dp', split_axis=0, concat_axis=0, tiled=True)  54.8 us
    all_gather x1, waiting for transfers between devices, shards(): lax.all_gather(query_key_value_weight, 'mp', axis=1, tiled=True)  46.9 us
    all_to_all x1, waiting for transfers between devices, shards(): lax.all_to_all(produced, 'dp', split_axis=0, concat_axis=0, tiled=True)  41.7 us
    sub x2, other arithmetic, shards(): expd = jnp.exp(scores - row_max)  27.1 us
    all_gather x1, blocking collectives, shards(): lax.all_gather(adapter_down_weight, 'dp', axis=0, tiled=True)  25.1 us
    all_gather x1, blocking collectives, shards(): lax.all_gather(adapter_up_weight, 'dp', axis=0, tiled=True)  23.2 us
    dot_general x2, matrix products, shards(): jnp.einsum('tgs,sd->tgd', probs, v_head, preferred_element_type=jnp.float32)  10.7 us
    dot_general x2, matrix products, shards(): jnp.einsum('tgd,sd->tgs', q_head, k_head, preferred_element_type=jnp.floa...  10.2 us
  transfers between devices with their start and end apart: 4, of which 2 were waited for; matrix products, arithmetic and copies ran while one was open for 22% of the time, Pallas kernels for 0%

commit v1 on v0

--- a/solution.py
+++ b/solution.py
@@ -8,6 +8,32 @@
 CAP = 48
 eps = 1e-06
 neg_fill = -1e30
+
+
+def pass_modes(my_tile, peer_axis):
+    b_now, mat_out, g_now = (lax.axis_size(peer_axis), lax.axis_index(peer_axis), my_tile.shape[0])
+    steps_seen = []
+    for ix, i0 in enumerate(my_tile.shape):
+        steps_seen.append(i0 * b_now if ix == 0 else i0)
+    prior = lax.dynamic_update_slice_in_dim(
+        jnp.zeros(steps_seen, my_tile.dtype), my_tile, mat_out * g_now, axis=0
+    )
+    w1 = upper = my_tile
+    for kk in range(1, b_now // 2 + 1):
+        history = []
+        for ix in range(b_now):
+            history.append((ix, (ix + 1) % b_now))
+        w1 = lax.ppermute(w1, peer_axis, history)
+        prior = lax.dynamic_update_slice_in_dim(prior, w1, (mat_out - kk) % b_now * g_now, axis=0)
+        if 2 * kk < b_now:
+            sheets = []
+            for ix in range(b_now):
+                sheets.append((ix, (ix - 1) % b_now))
+            upper = lax.ppermute(upper, peer_axis, sheets)
+            prior = lax.dynamic_update_slice_in_dim(
+                prior, upper, (mat_out + kk) % b_now * g_now, axis=0
+            )
+    return prior
 
 
 def rms_norm(values, gains):
@@ -39,7 +65,7 @@
     expert_down_weight,
 ):
     adapter_down_map, adapter_up_map = (
-        lax.all_gather(adapter_down_weight, "dp", axis=0, tiled=True),
+        pass_modes(adapter_down_weight, "dp"),
         lax.all_gather(adapter_up_weight, "dp", axis=0, tiled=True),
     )
     tokens_per_shard = tokens.shape[0]

time: 365 us -> 391 us (1.071)
  the two profiles are of different devices: /device:TPU:6 before, /device:TPU:2 now
where the time goes in v1:
time: 391 us; the launch traced here: 383 us
  waiting for transfers between devices  108 us (28%)
  blocking collectives  71.9 us (18%)
  matrix products  49 us (13%)
  other arithmetic  48.8 us (12%)
  local copies, waits for them, and re-layouts  47.7 us (12%)
  starting transfers between devices  43 us (11%)
  between operations  14.7 us (4%)
    all_to_all x1, blocking collectives, shards(): lax.all_to_all(outgoing, 'dp', split_axis=0, concat_axis=0, tiled=True)  48.9 us
    all_gather x1, waiting for transfers between devices, shards(): lax.all_gather(query_key_value_weight, 'mp', axis=1, tiled=True)  47.5 us
    all_to_all x1, waiting for transfers between devices, shards(): lax.all_to_all(produced, 'dp', split_axis=0, concat_axis=0, tiled=True)  39.7 us
    ppermute x7, starting transfers between devices, pass_modes(): upper = lax.ppermute(upper, peer_axis, sheets)  35.6 us
    sub x2, other arithmetic, shards(): expd = jnp.exp(scores - row_max)  26.6 us
    all_gather x1, blocking collectives, shards(): lax.all_gather(adapter_up_weight, 'dp', axis=0, tiled=True)  23 us
    ppermute x8, waiting for transfers between devices, pass_modes(): w1 = lax.ppermute(w1, peer_axis, history)  20.1 us
    dot_general x2, matrix products, shards(): jnp.einsum('tgs,sd->tgd', probs, v_head, preferred_element_type=jnp.float32)  10.7 us
  transfers between devices with their start and end apart: 19, of which 9 were waited for; matrix products, arithmetic and copies ran while one was open for 20% of the time, Pallas kernels for 0%

profile of v1, /device:TPU:2, one launch (start us, length us, event | category | flops | bytes accessed | tf_op | source)
XLA Modules:
  0.0 383.2 jit_solution(9433456072929827761)
XLA Ops:
  9.4 47.5 %all-gather.4.cloned.1.call-done = bf16[1536,2048]{1,0:T(8,128)(2,1)} async-done(((bf16[1536,256]{1,0:T(8,128)(2,1)}), bf16[1536,2048]{1,0:T(8,128)(2,1)}) %all-gather.4.cloned.1.call-update) | async-done | bytes 6291472 | tf_op jit(solution)/shard_map/all_gather | solution.py:79
  56.9 4.9 %fusion.49 = f32[256,2048]{1,0:T(8,128)S(1)} fusion(bf16[1536,2048]{1,0:T(8,128)(2,1)} %all-gather.4.cloned.1.call-done, bf16[256,1536]{1,0:T(8,128)(2,1)} %param.14, f32[1536]{0:T(1024)} %param.19, f32[256]{0:T(256)S(1)} %add_rsqrt_fusion.1), kind=kOutput, calls=%fused_computation.68 | convolution fusion | flops 1612185600 | bytes 9182208 | tf_op jit(solution)/shard_map/dot_general | solution.py:82
  71.8 9.0 %reduce-window.19 = s32[32,8,128]{2,1,0:T(8,128)S(1)} reduce-window(s32[32,8,128]{2,1,0:T(8,128)S(1)} %fusion.54, s32[]{:T(128)} %constant.133.clone.1), window={size=1x1x128 pad=0_0x0_0x127_0}, to_apply=%region_9.10 | reduce-window | flops 4161536 | bytes 262148 | tf_op jit(solution)/shard_map/reduce-window.1
  82.3 23.0 %all_gather.13 = bf16[16,16,1536]{2,1,0:T(8,128)(2,1)S(1)} all-gather(bf16[1,16,1536]{2,1,0:T(8,128)(2,1)S(1)} %copy-done.9), channel_id=1, replica_groups=mesh['dp'=16,'mp'=8] {'dp'}, dimensions={0}, use_global_device_ids=true | all-gather | bytes 835584 | tf_op jit(solution)/shard_map/all_gather | solution.py:69
  105.9 5.0 %collective-permute-start.3 = (bf16[1,1536,16]{1,2,0:T(8,128)(2,1)S(1)}, bf16[1,1536,16]{1,2,0:T(8,128)(2,1)S(1)}, u32[]{:S(2)}, u32[]{:S(2)}) collective-permute-start(bf16[1,1536,16]{1,2,0:T(8,128)(2,1)S(1)} %collective-permute-done.1), channel_id=1, source_target_pairs={{0,120},{8,0},{16,8},{24,16},{32,24},{40,32},{48,40},{56,48},{64,5... | collective-permute-start | bytes 147464 | tf_op jit(solution)/shard_map/ppermute | solution.py:32
  113.4 5.3 %collective-permute-start.5 = (bf16[1,1536,16]{1,2,0:T(8,128)(2,1)S(1)}, bf16[1,1536,16]{1,2,0:T(8,128)(2,1)S(1)}, u32[]{:S(2)}, u32[]{:S(2)}) collective-permute-start(bf16[1,1536,16]{1,2,0:T(8,128)(2,1)S(1)} %collective-permute-done.3), channel_id=1, source_target_pairs={{0,120},{8,0},{16,8},{24,16},{32,24},{40,32},{48,40},{56,48},{64,5... | collective-permute-start | bytes 147464 | tf_op jit(solution)/shard_map/ppermute | solution.py:32
  120.8 5.3 %collective-permute-start.7 = (bf16[1,1536,16]{1,2,0:T(8,128)(2,1)S(1)}, bf16[1,1536,16]{1,2,0:T(8,128)(2,1)S(1)}, u32[]{:S(2)}, u32[]{:S(2)}) collective-permute-start(bf16[1,1536,16]{1,2,0:T(8,128)(2,1)S(1)} %collective-permute-done.5), channel_id=1, source_target_pairs={{0,120},{8,0},{16,8},{24,16},{32,24},{40,32},{48,40},{56,48},{64,5... | collective-permute-start | bytes 147464 | tf_op jit(solution)/shard_map/ppermute | solution.py:32
  128.3 5.3 %collective-permute-start.9 = (bf16[1,1536,16]{1,2,0:T(8,128)(2,1)S(1)}, bf16[1,1536,16]{1,2,0:T(8,128)(2,1)S(1)}, u32[]{:S(2)}, u32[]{:S(2)}) collective-permute-start(bf16[1,1536,16]{1,2,0:T(8,128)(2,1)S(1)} %collective-permute-done.7), channel_id=1, source_target_pairs={{0,120},{8,0},{16,8},{24,16},{32,24},{40,32},{48,40},{56,48},{64,5... | collective-permute-start | bytes 147464 | tf_op jit(solution)/shard_map/ppermute | solution.py:32
  135.7 5.3 %collective-permute-start.11 = (bf16[1,1536,16]{1,2,0:T(8,128)(2,1)S(1)}, bf16[1,1536,16]{1,2,0:T(8,128)(2,1)S(1)}, u32[]{:S(2)}, u32[]{:S(2)}) collective-permute-start(bf16[1,1536,16]{1,2,0:T(8,128)(2,1)S(1)} %collective-permute-done.9), channel_id=1, source_target_pairs={{0,120},{8,0},{16,8},{24,16},{32,24},{40,32},{48,40},{56,48},{64,5... | collective-permute-start | bytes 147464 | tf_op jit(solution)/shard_map/ppermute | solution.py:32
  143.1 5.3 %collective-permute-start.13 = (bf16[1,1536,16]{1,2,0:T(8,128)(2,1)S(1)}, bf16[1,1536,16]{1,2,0:T(8,128)(2,1)S(1)}, u32[]{:S(2)}, u32[]{:S(2)}) collective-permute-start(bf16[1,1536,16]{1,2,0:T(8,128)(2,1)S(1)} %collective-permute-done.11), channel_id=1, source_target_pairs={{0,120},{8,0},{16,8},{24,16},{32,24},{40,32},{48,40},{56,48},{64,5... | collective-permute-start | bytes 147464 | tf_op jit(solution)/shard_map/ppermute | solution.py:32
  151.0 7.3 %collective-permute-done.14 = bf16[1,1536,16]{1,2,0:T(8,128)(2,1)S(1)} collective-permute-done((bf16[1,1536,16]{1,2,0:T(8,128)(2,1)S(1)}, bf16[1,1536,16]{1,2,0:T(8,128)(2,1)S(1)}, u32[]{:S(2)}, u32[]{:S(2)}) %collective-permute-start.14) | collective-permute-done | bytes 49184 | tf_op jit(solution)/shard_map/ppermute | solution.py:26
  161.4 7.3 %fusion.46 = f32[256,6,2048]{2,0,1:T(8,128)} fusion(bf16[256,6,128]{0,2,1:T(8,128)(2,1)S(1)} %bitcast.93, bf16[2048,512]{1,0:T(8,128)(2,1)} %all-gather.6.cloned.1.call-done), kind=kOutput, calls=%fused_computation.66 | convolution fusion | flops 805306368 | bytes 13500416 | tf_op jit(solution)/shard_map/tgd,sd->tgs/dot_general | solution.py:131
  171.6 17.2 %fusion.70 = (f32[256,6]{0,1:T(8,128)S(1)}, f32[256,6,2048]{2,0,1:T(8,128)}) fusion(f32[256,6,2048]{2,0,1:T(8,128)} %fusion.46, pred[256,2048]{1,0:T(8,128)(4,1)} %fusion.31), kind=kOutput, calls=%fused_computation.128 | output fusion | flops 18876416 | bytes 25696256 | tf_op jit(solution)/shard_map/sub | solution.py:136
  188.8 9.5 %fusion.69 = (f32[256,6]{0,1:T(8,128)S(1)}, f32[256,6,2048]{2,0,1:T(8,128)}) fusion(f32[256,6,2048]{2,0,1:T(8,128)S(1)} %fusion.45, pred[256,2048]{1,0:T(8,128)(4,1)} %fusion.31), kind=kOutput, calls=%fused_computation.127 | output fusion | flops 18876416 | bytes 25696256 | tf_op jit(solution)/shard_map/sub | solution.py:136
  198.3 7.0 %fusion.36 = bf16[256,6,128]{0,2,1:T(8,128)(2,1)S(1)} fusion(f32[256,6,2048]{2,0,1:T(8,128)} %get-tuple-element.9, f32[256,6]{0,1:T(8,128)S(1)} %get-tuple-element.8, bf16[2048,512]{1,0:T(8,128)(2,1)} %all-gather.6.cloned.1.call-done), kind=kOutput, calls=%fused_computation.53 | convolution fusion | flops 811794432 | bytes 13506560 | tf_op jit(solution)/shard_map/tgs,sd->tgd/dot_general | solution.py:138
  219.9 9.2 %scatter_custom_fusion = bf16[1536,1536]{1,0:T(8,128)(2,1)} fusion(s32[1024]{0:T(1024)S(1)} %bitcast.99, bf16[1024,1536]{1,0:T(8,128)(2,1)} %reshape.285, bf16[]{:T(256)} %constant.137.clone.1), kind=kCustom, calls=%fused_computation.42 | custom fusion | bytes 4719104 | tf_op jit(solution)/shard_map/scatter | solution.py:164
  229.1 48.9 %all_to_all.10 = bf16[16,2,48,1536]{3,2,1,0:T(8,128)(2,1)S(1)} all-to-all(bf16[16,2,48,1536]{3,2,1,0:T(8,128)(2,1)} %bitcast.92), channel_id=1, replica_groups=mesh['dp'=16,'mp'=8] {'dp'}, dimensions={0} | all-to-all | bytes 9437184 | tf_op jit(solution)/shard_map/all_to_all | solution.py:169
  278.0 10.0 %fusion.14 = f32[16,2,48,1536]{3,2,0,1:T(8,128)S(1)} fusion(bf16[2,1536,1536]{2,1,0:T(8,128)(2,1)} %param.26, bf16[16,2,48,1536]{3,2,1,0:T(8,128)(2,1)S(1)} %all_to_all.10), kind=kOutput, calls=%fused_computation.25 | convolution fusion | flops 7247757312 | bytes 23592960 | tf_op jit(solution)/shard_map/secd,edf->secf/dot_general | solution.py:170
  288.0 6.4 %convert_bitcast_fusion = bf16[16,2,48,1536]{3,2,0,1:T(8,128)(2,1)S(1)} fusion(bf16[2,768,1536]{2,1,0:T(8,128)(2,1)} %param.27, f32[16,2,48,1536]{3,2,0,1:T(8,128)S(1)} %fusion.14), kind=kOutput, calls=%fused_computation.32 | convolution fusion | flops 3629776896 | bytes 18874368 | tf_op jit(solution)/shard_map/secf,efd->secd/dot_general | solution.py:177
  296.9 4.9 %all-to-all-start.1 = ((bf16[16,2,48,1536]{3,2,1,0:T(8,128)(2,1)}), bf16[16,2,48,1536]{3,2,1,0:T(8,128)(2,1)}, u32[]{:S(2)}, u32[]{:S(2)}) async-start(bf16[16,2,48,1536]{3,2,1,0:T(8,128)(2,1)} %copy.87), calls=%async_computation.1 | async-start | bytes 9437184 | tf_op jit(solution)/shard_map/all_to_all | solution.py:180
  302.7 8.7 %gather_fusion.2 = f32[1024]{0:T(1024)S(1)} fusion(f32[256,32]{0,1:T(8,128)S(1)} %fusion.71, s32[1024]{0:T(1024)S(1)} %reshape.275), kind=kCustom, calls=%fused_computation.2 | custom fusion | bytes 16384 | tf_op jit(solution)/shard_map/jit(take_along_axis)/gather | solution.py:151
  314.7 39.7 %all-to-all-done.1 = bf16[16,2,48,1536]{3,2,1,0:T(8,128)(2,1)} async-done(((bf16[16,2,48,1536]{3,2,1,0:T(8,128)(2,1)}), bf16[16,2,48,1536]{3,2,1,0:T(8,128)(2,1)}, u32[]{:S(2)}, u32[]{:S(2)}) %all-to-all-start.1) | async-done | bytes 4718624 | tf_op jit(solution)/shard_map/all_to_all | solution.py:180
  354.4 9.6 %gather_fusion = bf16[1024,1536]{1,0:T(8,128)(2,1)S(1)} fusion(bf16[1536,1536]{1,0:T(8,128)(2,1)} %bitcast.28, s32[1024]{0:T(1024)S(1)} %broadcast_clamp_fusion), kind=kCustom, calls=%fused_computation | custom fusion | bytes 6295552 | tf_op jit(solution)/shard_map/gather | solution.py:182
  367.9 7.5 %multiply_reduce_fusion = f32[256,1536]{1,0:T(8,128)S(1)} fusion(f32[256,4,1536]{2,1,0:T(4,128)} %reshape.258, f32[256,4]{1,0:T(8,128)S(1)} %copy.90), kind=kLoop, calls=%fused_computation.16 | loop fusion | flops 2752512 | bytes 7868416 | tf_op jit(solution)/shard_map/reduce_sum | solution.py:186
  (141 shorter events, 59.2 us)
Async XLA Ops:
  7.2 295.2 %copy-start = (bf16[1536,32]{0,1:T(8,128)(2,1)S(1)}, bf16[1536,32]{0,1:T(8,128)(2,1)}, u32[]{:S(2)}) copy-start(bf16[1536,32]{0,1:T(8,128)(2,1)} %param.25) | copy-start | bytes 294916
  7.2 49.7 %all-gather.4.cloned.1.call-start = ((), (), s32[]{:S(2)}) async-start(), calls=%async_computation.2 | async-start | bytes 7077888 | tf_op jit(solution)/shard_map/all_gather | solution.py:79
  7.9 153.5 %all-gather.6.cloned.1.call-start = ((), (), s32[]{:S(2)}) async-start(), calls=%async_computation.3 | async-start | bytes 2359296 | tf_op jit(solution)/shard_map/all_gather | solution.py:113
  9.4 60.5 %copy-start.16 = (s32[1,4]{1,0:T(1,128)S(1)}, s32[1,4]{1,0:T(1,128)}, u32[]{:S(2)}) copy-start(s32[1,4]{1,0:T(1,128)} %param.15) | copy-start | bytes 52
  9.4 60.8 %copy-start.14 = (s32[1,4]{1,0:T(1,128)S(1)}, s32[1,4]{1,0:T(1,128)}, u32[]{:S(2)}) copy-start(s32[1,4]{1,0:T(1,128)} %param.16) | copy-start | bytes 52
  63.1 95.2 %copy-start.5 = (bf16[256,1536]{1,0:T(8,128)(2,1)S(1)}, bf16[256,1536]{1,0:T(8,128)(2,1)}, u32[]{:S(2)}) copy-start(bf16[256,1536]{1,0:T(8,128)(2,1)} %param.14) | copy-start | bytes 2359300
  63.2 95.2 %copy-start.15 = (f32[1536]{0:T(1024)S(1)}, f32[1536]{0:T(1024)}, u32[]{:S(2)}) copy-start(f32[1536]{0:T(1024)} %param.19) | copy-start | bytes 18436
  63.9 146.4 %all-gather.8.cloned.1.call-start = ((), (), s32[]{:S(2)}) async-start(), calls=%async_computation.4 | async-start | bytes 5308416 | tf_op jit(solution)/shard_map/all_gather | solution.py:80
  64.0 41.5 %collective-permute-start = (bf16[1,1536,16]{1,2,0:T(8,128)(2,1)S(1)}, bf16[1,1536,16]{1,2,0:T(8,128)(2,1)S(1)}, u32[]{:S(2)}, u32[]{:S(2)}) collective-permute-start(bf16[1,1536,16]{1,2,0:T(8,128)(2,1)S(1)} %copy-done.10), channel_id=1, source_target_pairs={{0,8},{8,16},{16,24},{24,32},{32,40},{40,48},{48,56},{56,64},{64,7... | collective-permute-start | bytes 147464 | tf_op jit(solution)/shard_map/ppermute | solution.py:26
  65.5 40.4 %collective-permute-start.1 = (bf16[1,1536,16]{1,2,0:T(8,128)(2,1)S(1)}, bf16[1,1536,16]{1,2,0:T(8,128)(2,1)S(1)}, u32[]{:S(2)}, u32[]{:S(2)}) collective-permute-start(bf16[1,1536,16]{1,2,0:T(8,128)(2,1)S(1)} %copy-done.10), channel_id=1, source_target_pairs={{0,120},{8,0},{16,8},{24,16},{32,24},{40,32},{48,40},{56,48},{64,5... | collective-permute-start | bytes 147464 | tf_op jit(solution)/shard_map/ppermute | solution.py:32
  105.5 7.9 %collective-permute-start.2 = (bf16[1,1536,16]{1,2,0:T(8,128)(2,1)S(1)}, bf16[1,1536,16]{1,2,0:T(8,128)(2,1)S(1)}, u32[]{:S(2)}, u32[]{:S(2)}) collective-permute-start(bf16[1,1536,16]{1,2,0:T(8,128)(2,1)S(1)} %collective-permute-done), channel_id=1, source_target_pairs={{0,8},{8,16},{16,24},{24,32},{32,40},{40,48},{48,56},{56,64},{64,7... | collective-permute-start | bytes 147464 | tf_op jit(solution)/shard_map/ppermute | solution.py:26
  105.9 7.5 %collective-permute-start.3 = (bf16[1,1536,16]{1,2,0:T(8,128)(2,1)S(1)}, bf16[1,1536,16]{1,2,0:T(8,128)(2,1)S(1)}, u32[]{:S(2)}, u32[]{:S(2)}) collective-permute-start(bf16[1,1536,16]{1,2,0:T(8,128)(2,1)S(1)} %collective-permute-done.1), channel_id=1, source_target_pairs={{0,120},{8,0},{16,8},{24,16},{32,24},{40,32},{48,40},{56,48},{64,5... | collective-permute-start | bytes 147464 | tf_op jit(solution)/shard_map/ppermute | solution.py:32
  113.4 7.4 %collective-permute-start.4 = (bf16[1,1536,16]{1,2,0:T(8,128)(2,1)S(1)}, bf16[1,1536,16]{1,2,0:T(8,128)(2,1)S(1)}, u32[]{:S(2)}, u32[]{:S(2)}) collective-permute-start(bf16[1,1536,16]{1,2,0:T(8,128)(2,1)S(1)} %collective-permute-done.2), channel_id=1, source_target_pairs={{0,8},{8,16},{16,24},{24,32},{32,40},{40,48},{48,56},{56,64},{64,7... | collective-permute-start | bytes 147464 | tf_op jit(solution)/shard_map/ppermute | solution.py:26
  113.4 7.4 %collective-permute-start.5 = (bf16[1,1536,16]{1,2,0:T(8,128)(2,1)S(1)}, bf16[1,1536,16]{1,2,0:T(8,128)(2,1)S(1)}, u32[]{:S(2)}, u32[]{:S(2)}) collective-permute-start(bf16[1,1536,16]{1,2,0:T(8,128)(2,1)S(1)} %collective-permute-done.3), channel_id=1, source_target_pairs={{0,120},{8,0},{16,8},{24,16},{32,24},{40,32},{48,40},{56,48},{64,5... | collective-permute-start | bytes 147464 | tf_op jit(solution)/shard_map/ppermute | solution.py:32
  120.8 7.4 %collective-permute-start.6 = (bf16[1,1536,16]{1,2,0:T(8,128)(2,1)S(1)}, bf16[1,1536,16]{1,2,0:T(8,128)(2,1)S(1)}, u32[]{:S(2)}, u32[]{:S(2)}) collective-permute-start(bf16[1,1536,16]{1,2,0:T(8,128)(2,1)S(1)} %collective-permute-done.4), channel_id=1, source_target_pairs={{0,8},{8,16},{16,24},{24,32},{32,40},{40,48},{48,56},{56,64},{64,7... | collective-permute-start | bytes 147464 | tf_op jit(solution)/shard_map/ppermute | solution.py:26
  120.8 7.4 %collective-permute-start.7 = (bf16[1,1536,16]{1,2,0:T(8,128)(2,1)S(1)}, bf16[1,1536,16]{1,2,0:T(8,128)(2,1)S(1)}, u32[]{:S(2)}, u32[]{:S(2)}) collective-permute-start(bf16[1,1536,16]{1,2,0:T(8,128)(2,1)S(1)} %collective-permute-done.5), channel_id=1, source_target_pairs={{0,120},{8,0},{16,8},{24,16},{32,24},{40,32},{48,40},{56,48},{64,5... | collective-permute-start | bytes 147464 | tf_op jit(solution)/shard_map/ppermute | solution.py:32
  128.3 7.4 %collective-permute-start.8 = (bf16[1,1536,16]{1,2,0:T(8,128)(2,1)S(1)}, bf16[1,1536,16]{1,2,0:T(8,128)(2,1)S(1)}, u32[]{:S(2)}, u32[]{:S(2)}) collective-permute-start(bf16[1,1536,16]{1,2,0:T(8,128)(2,1)S(1)} %collective-permute-done.6), channel_id=1, source_target_pairs={{0,8},{8,16},{16,24},{24,32},{32,40},{40,48},{48,56},{56,64},{64,7... | collective-permute-start | bytes 147464 | tf_op jit(solution)/shard_map/ppermute | solution.py:26
  128.3 7.4 %collective-permute-start.9 = (bf16[1,1536,16]{1,2,0:T(8,128)(2,1)S(1)}, bf16[1,1536,16]{1,2,0:T(8,128)(2,1)S(1)}, u32[]{:S(2)}, u32[]{:S(2)}) collective-permute-start(bf16[1,1536,16]{1,2,0:T(8,128)(2,1)S(1)} %collective-permute-done.7), channel_id=1, source_target_pairs={{0,120},{8,0},{16,8},{24,16},{32,24},{40,32},{48,40},{56,48},{64,5... | collective-permute-start | bytes 147464 | tf_op jit(solution)/shard_map/ppermute | solution.py:32
  135.7 7.4 %collective-permute-start.10 = (bf16[1,1536,16]{1,2,0:T(8,128)(2,1)S(1)}, bf16[1,1536,16]{1,2,0:T(8,128)(2,1)S(1)}, u32[]{:S(2)}, u32[]{:S(2)}) collective-permute-start(bf16[1,1536,16]{1,2,0:T(8,128)(2,1)S(1)} %collective-permute-done.8), channel_id=1, source_target_pairs={{0,8},{8,16},{16,24},{24,32},{32,40},{40,48},{48,56},{56,64},{64,7... | collective-permute-start | bytes 147464 | tf_op jit(solution)/shard_map/ppermute | solution.py:26
  135.7 7.4 %collective-permute-start.11 = (bf16[1,1536,16]{1,2,0:T(8,128)(2,1)S(1)}, bf16[1,1536,16]{1,2,0:T(8,128)(2,1)S(1)}, u32[]{:S(2)}, u32[]{:S(2)}) collective-permute-start(bf16[1,1536,16]{1,2,0:T(8,128)(2,1)S(1)} %collective-permute-done.9), channel_id=1, source_target_pairs={{0,120},{8,0},{16,8},{24,16},{32,24},{40,32},{48,40},{56,48},{64,5... | collective-permute-start | bytes 147464 | tf_op jit(solution)/shard_map/ppermute | solution.py:32
  143.1 7.4 %collective-permute-start.12 = (bf16[1,1536,16]{1,2,0:T(8,128)(2,1)S(1)}, bf16[1,1536,16]{1,2,0:T(8,128)(2,1)S(1)}, u32[]{:S(2)}, u32[]{:S(2)}) collective-permute-start(bf16[1,1536,16]{1,2,0:T(8,128)(2,1)S(1)} %collective-permute-done.10), channel_id=1, source_target_pairs={{0,8},{8,16},{16,24},{24,32},{32,40},{40,48},{48,56},{56,64},{64,7... | collective-permute-start | bytes 147464 | tf_op jit(solution)/shard_map/ppermute | solution.py:26
  143.1 7.9 %collective-permute-start.13 = (bf16[1,1536,16]{1,2,0:T(8,128)(2,1)S(1)}, bf16[1,1536,16]{1,2,0:T(8,128)(2,1)S(1)}, u32[]{:S(2)}, u32[]{:S(2)}) collective-permute-start(bf16[1,1536,16]{1,2,0:T(8,128)(2,1)S(1)} %collective-permute-done.11), channel_id=1, source_target_pairs={{0,120},{8,0},{16,8},{24,16},{32,24},{40,32},{48,40},{56,48},{64,5... | collective-permute-start | bytes 147464 | tf_op jit(solution)/shard_map/ppermute | solution.py:32
  150.5 7.9 %collective-permute-start.14 = (bf16[1,1536,16]{1,2,0:T(8,128)(2,1)S(1)}, bf16[1,1536,16]{1,2,0:T(8,128)(2,1)S(1)}, u32[]{:S(2)}, u32[]{:S(2)}) collective-permute-start(bf16[1,1536,16]{1,2,0:T(8,128)(2,1)S(1)} %collective-permute-done.12), channel_id=1, source_target_pairs={{0,8},{8,16},{16,24},{24,32},{32,40},{40,48},{48,56},{56,64},{64,7... | collective-permute-start | bytes 147464 | tf_op jit(solution)/shard_map/ppermute | solution.py:26
  296.9 57.5 %all-to-all-start.1 = ((bf16[16,2,48,1536]{3,2,1,0:T(8,128)(2,1)}), bf16[16,2,48,1536]{3,2,1,0:T(8,128)(2,1)}, u32[]{:S(2)}, u32[]{:S(2)}) async-start(bf16[16,2,48,1536]{3,2,1,0:T(8,128)(2,1)} %copy.87), calls=%async_computation.1 | async-start | bytes 9437184 | tf_op jit(solution)/shard_map/all_to_all | solution.py:180
  (14 other events, 181.0 us)
Sparse Core Ops, SparseCore 0:
  9.7 47.1 all-gather.3
  64.0 25.3 all-gather.5
  91.1 34.4 all-gather.7
